TPU v7x, 256 devices: a whole 4x4x8 slice. The times are simulated.
256 devices in a mesh: layer: 8 (over x, y_hi), feat: 32 (over y_lo, z, core).
Axes of the slice: x: 4, y: 4 (y_hi: 2, y_lo: 2; y = y_hi * 2 + y_lo), z: 8, core: 2. Of those that a mesh axis runs over, the one named last changes fastest.
Arguments:
- inputs: bfloat16 [8, 512, 2048], P('layer', 'feat'), may hold values from -6 to 6
- targets: bfloat16 [8, 512, 2048], P('layer', 'feat'), may hold values from -6 to 6
- enc_weight: bfloat16 [8, 2048, 16384], P('layer', None, 'feat'), may hold values from -0.125 to 0.125
- enc_bias: float32 [8, 16384], P('layer', 'feat'), may hold values from -1 to 0.5
- dec_weight: bfloat16 [8, 2, 16384, 2048], P('layer', None, 'feat'), may hold values from -0.046875 to 0.046875
- dec_bias: float32 [8, 2048], P('layer'), may hold values from -3 to 3
Outputs:
- mean_loss: float32 [], replicated
- enc_grad: bfloat16 [8, 2048, 16384], P('layer', None, 'feat')
- enc_bias_grad: float32 [8, 16384], P('layer', 'feat')
- dec_grad: bfloat16 [8, 2, 16384, 2048], P('layer', None, 'feat')
- dec_bias_grad: float32 [8, 2048], P('layer')
All inputs are finite; a program needn't handle non-finite values.
Results may differ from a plain program's by a relative error of at most 0.006.
Values may be sent and summed in bfloat16 or wider, within the bound.
A program may use at most 128 MiB of HBM per device.

v0:
```python
import functools
import jax
import jax.numpy as jnp
from jax import lax
from jax.sharding import Mesh
from jax.sharding import PartitionSpec as P

FEAT = ("feat_0", "feat_1", "feat_2")
LAYER = ("layer_0", "layer_1")
LAYER_FEAT = ("layer_0", "layer_1", "feat_0", "feat_1", "feat_2")


def copy_for_each(value, axis):
    size = lax.axis_size(axis)
    return lax.all_to_all(
        jnp.broadcast_to(value[None], (size, *value.shape)), axis, 0, 0, tiled=True
    )


def joined_along(tiles, dim):
    lengths = list(tiles.shape[1:])
    lengths[dim] *= tiles.shape[0]
    return jnp.moveaxis(tiles, 0, dim).reshape(lengths)


def collect(value, axis, dim):
    tiles = copy_for_each(value, axis)
    return joined_along(tiles, dim)


def cut_along(value, dim, size):
    lengths = value.shape
    tiles = value.reshape(*lengths[:dim], size, lengths[dim] // size, *lengths[dim + 1 :])
    return jnp.moveaxis(tiles, dim, 0)


def scatter_pairs(value, chips, core, dim):
    sizes = (lax.axis_size(chips), lax.axis_size(core))
    tiles = cut_along(value, dim, sizes[0] * sizes[1])
    inside = tiles.shape[1:]
    tiles = tiles.reshape(*sizes, *inside).swapaxes(0, 1).reshape(-1, *inside)
    tiles = lax.psum_scatter(tiles, core, scatter_dimension=0, tiled=True)
    return lax.psum_scatter(tiles, chips, scatter_dimension=0, tiled=True)[0]


def passed_along(block, axis, distance):
    devices = range(lax.axis_size(axis))
    route = [(i - distance, i) for i in devices if i - distance in devices]
    return lax.ppermute(block, axis, route)


def one_axis_at_a_time(value, axes):
    return functools.reduce(lax.psum, axes, value)


def shards(inputs, targets, enc_weight, enc_bias, dec_weight, dec_bias):
    shard_rows = inputs.shape[1]
    reach = dec_weight.shape[1]
    width = dec_weight.shape[3]
    tokens_all = collect(inputs[0], FEAT, 0)
    pre = jnp.dot(tokens_all, enc_weight[0], preferred_element_type=jnp.float32) + enc_bias[0]
    acts = (jnp.maximum(pre, 0.0) ** 2).astype(jnp.bfloat16)
    out = jnp.einsum("tf,rfd->trd", acts, dec_weight[0], preferred_element_type=jnp.float32)
    summed = scatter_pairs(
        out.reshape(
            shard_rows * lax.axis_size(("feat_0", "feat_1")) * lax.axis_size("feat_2"),
            reach * width,
        ),
        ("feat_0", "feat_1"),
        "feat_2",
        0,
    )
    recon = summed[:, :width] + dec_bias[0]
    offset = 1
    recon = recon + passed_along(summed[:, offset * width : (offset + 1) * width], LAYER, offset)
    grad = (recon - targets[0].astype(jnp.float32)).astype(jnp.bfloat16)
    local_squares = jnp.sum(grad.astype(jnp.float32) ** 2)
    total = one_axis_at_a_time(local_squares, LAYER_FEAT)
    mean_loss = total / (lax.axis_size(LAYER) * lax.axis_size(FEAT) * shard_rows * width)
    pieces = [grad]
    offset = 1
    pieces.append(passed_along(grad, LAYER, -offset))
    stacked = jnp.stack(pieces, axis=1)
    gathered = lax.all_gather(stacked, FEAT, axis=0, tiled=True)
    fulls = [gathered[:, offset] for offset in range(reach)]
    dec_parts = []
    back = jnp.zeros(pre.shape, jnp.float32)
    for offset in range(reach):
        dec_parts.append(
            jnp.einsum("tf,td->fd", acts, fulls[offset], preferred_element_type=jnp.float32).astype(
                jnp.bfloat16
            )
        )
        back = back + jnp.einsum(
            "td,fd->tf", fulls[offset], dec_weight[0, offset], preferred_element_type=jnp.float32
        )
    dec_grad = jnp.stack(dec_parts, axis=0)
    dpre = (back * 2.0 * jnp.maximum(pre, 0.0)).astype(jnp.bfloat16)
    enc_grad = jnp.einsum("td,tf->df", tokens_all, dpre, preferred_element_type=jnp.float32).astype(
        jnp.bfloat16
    )
    enc_bias_grad = jnp.sum(dpre.astype(jnp.float32), axis=0)
    dec_bias_grad = jnp.sum(fulls[0].astype(jnp.float32), axis=0)
    return (mean_loss, enc_grad[None], enc_bias_grad[None], dec_grad[None], dec_bias_grad[None])


def solution(mesh):
    finer = Mesh(
        mesh.devices.reshape(4, 2, 2, 8, 2), ("layer_0", "layer_1", "feat_0", "feat_1", "feat_2")
    )
    placed = (
        P(LAYER, FEAT, None),
        P(LAYER, FEAT, None),
        P(LAYER, None, FEAT),
        P(LAYER, FEAT),
        P(LAYER, None, FEAT, None),
        P(LAYER, None),
    )
    return jax.shard_map(
        shards,
        mesh=finer,
        in_specs=placed,
        out_specs=(
            P(),
            P(LAYER, None, FEAT),
            P(LAYER, FEAT),
            P(LAYER, None, FEAT, None),
            P(LAYER, None),
        ),
        check_vma=False,
    )
```

profile of v0, /device:TPU:1, one launch (start us, length us, event | category | flops | bytes accessed | tf_op | source)
XLA Modules:
  0.0 300.6 jit_solution(5352324902528373081)
XLA Ops:
  7.2 0.0 copy-start
  7.2 2.6 broadcast_in_dim.20
  9.7 11.2 %all-to-all-start = ((bf16[32,16,2048]{2,1,0:T(8,128)(2,1)}), bf16[32,16,2048]{2,1,0:T(8,128)(2,1)}, u32[]{:S(2)}, u32[]{:S(2)}) async-start(bf16[32,16,2048]{2,1,0:T(8,128)(2,1)} %broadcast_in_dim.20), calls=%async_computation | async-start | bytes 4194304 | tf_op jit(solution)/shard_map/all_to_all | solution.py:15
  20.9 0.0 copy-start.7
  20.9 0.0 reduce-scatter.3.cloned.1.call-start
  21.0 6.2 %copy.12 = bf16[1,2,512,2048]{2,3,1,0:T(8,128)(2,1)} copy(bf16[1,2,512,2048]{3,2,1,0:T(8,128)(2,1)} %param.10) | data formatting | bytes 8388608 | tf_op args[4]
  27.2 43.0 %all-to-all-done = bf16[32,16,2048]{2,1,0:T(8,128)(2,1)} async-done(((bf16[32,16,2048]{2,1,0:T(8,128)(2,1)}), bf16[32,16,2048]{2,1,0:T(8,128)(2,1)}, u32[]{:S(2)}, u32[]{:S(2)}) %all-to-all-start) | async-done | bytes 2097184 | tf_op jit(solution)/shard_map/all_to_all | solution.py:15
  70.2 0.0 copy-done
  70.2 0.0 copy-done.7
  70.2 0.0 copy-start.2
  70.2 4.0 %multiply_convert_fusion = (bf16[512,512]{1,0:T(8,128)(2,1)S(1)}, f32[512,512]{1,0:T(8,128)}) fusion(f32[512]{0:T(512)S(1)} %bitcast.97, bf16[512,2048]{1,0:T(8,128)(2,1)} %bitcast.1, bf16[1,2048,512]{2,1,0:T(8,128)(2,1)S(1)} %copy-done), kind=kOutput, calls=%fused_computation.26 | convolution fusion | flops 1074790400 | bytes 5769216 | tf_op jit(solution)/shard_map/dot_general | solution.py:61
  74.2 0.0 copy-done.2
  74.2 2.4 convolution_bitcast_fusion
  76.6 3.8 %copy.13 = f32[2,16,16,4096]{3,2,1,0:T(8,128)} copy(f32[2,16,16,4096]{3,2,0,1:T(8,128)S(1)} %convolution_bitcast_fusion) | data formatting | bytes 16777216 | tf_op jit(solution)/shard_map/transpose | solution.py:41
  80.4 0.0 reduce-scatter.3.cloned.1.call-update
  80.4 0.0 reduce-scatter.5.cloned.1.call-start
  80.5 21.5 %reduce-scatter.3.cloned.1.call-done = f32[16,16,4096]{2,1,0:T(8,128)} async-done(((f32[32,16,4096]{2,1,0:T(8,128)}), f32[16,16,4096]{2,1,0:T(8,128)}) %reduce-scatter.3.cloned.1.call-update) | async-done | bytes 4194320 | tf_op jit(solution)/shard_map/reduce_scatter | solution.py:42
  102.0 0.0 reduce-scatter.5.cloned.1.call-update
  102.0 0.0 all-gather.2.cloned.1.call-start
  102.1 74.0 %reduce-scatter.5.cloned.1.call-done = f32[1,16,4096]{2,1,0:T(8,128)} async-done(((f32[16,16,4096]{2,1,0:T(8,128)}), f32[1,16,4096]{2,1,0:T(8,128)}) %reduce-scatter.5.cloned.1.call-update) | async-done | bytes 262160 | tf_op jit(solution)/shard_map/reduce_scatter | solution.py:43
  176.0 0.9 slice.25
  176.9 4.4 %collective-permute-start = (f32[16,2048]{1,0:T(8,128)S(1)}, f32[16,2048]{1,0:T(8,128)S(1)}, u32[]{:S(2)}, u32[]{:S(2)}) collective-permute-start(f32[16,2048]{1,0:T(8,128)S(1)} %slice.25), channel_id=1, source_target_pairs={{0,32},{32,64},{64,96},{96,128},{128,160},{160,192},{192,224},{1,3... | collective-permute-start | bytes 393224 | tf_op jit(solution)/shard_map/ppermute | solution.py:49
  181.3 3.3 %collective-permute-done = f32[16,2048]{1,0:T(8,128)S(1)} collective-permute-done((f32[16,2048]{1,0:T(8,128)S(1)}, f32[16,2048]{1,0:T(8,128)S(1)}, u32[]{:S(2)}, u32[]{:S(2)}) %collective-permute-start) | collective-permute-done | bytes 131104 | tf_op jit(solution)/shard_map/ppermute | solution.py:49
  184.6 0.0 copy-done.5
  184.6 0.0 copy-done.6
  184.6 1.6 multiply_reduce_fusion
  186.2 1.3 collective-permute-start.1
  187.5 6.1 %collective-permute-done.1 = bf16[16,2048]{1,0:T(8,128)(2,1)S(1)} collective-permute-done((bf16[16,2048]{1,0:T(8,128)(2,1)S(1)}, bf16[16,2048]{1,0:T(8,128)(2,1)S(1)}, u32[]{:S(2)}, u32[]{:S(2)}) %collective-permute-start.1) | collective-permute-done | bytes 65568 | tf_op jit(solution)/shard_map/ppermute | solution.py:49
  193.5 0.7 pad_maximum_fusion
  194.2 0.0 all-gather.2.cloned.1.call-update
  194.2 9.7 %psum.35 = f32[]{:T(128)} all-reduce(f32[]{:T(128)} %get-tuple-element.15), channel_id=1, replica_groups=mesh['layer_0'=4,'layer_1'=2,'feat_0'=2,'feat_1'=8,'feat_2'=2] {'layer_0'}, use_global_device_ids=true, to_apply=%region_3.0 | all-reduce | flops 1 | bytes 8 | tf_op jit(solution)/shard_map/psum | solution.py:53
  203.9 5.9 %psum.36 = f32[]{:T(128)} all-reduce(f32[]{:T(128)} %psum.35), channel_id=1, replica_groups=mesh['layer_0'=4,'layer_1'=2,'feat_0'=2,'feat_1'=8,'feat_2'=2] {'layer_1'}, use_global_device_ids=true, to_apply=%region_4.0 | all-reduce | flops 1 | bytes 8 | tf_op jit(solution)/shard_map/psum | solution.py:53
  209.8 4.4 %psum.37 = f32[]{:T(128)} all-reduce(f32[]{:T(128)} %psum.36), channel_id=1, replica_groups=mesh['layer_0'=4,'layer_1'=2,'feat_0'=2,'feat_1'=8,'feat_2'=2] {'feat_0'}, use_global_device_ids=true, to_apply=%region_5.0 | all-reduce | flops 1 | bytes 8 | tf_op jit(solution)/shard_map/psum | solution.py:53
  214.2 11.8 %psum.38 = f32[]{:T(128)} all-reduce(f32[]{:T(128)} %psum.37), channel_id=1, replica_groups=mesh['layer_0'=4,'layer_1'=2,'feat_0'=2,'feat_1'=8,'feat_2'=2] {'feat_1'}, use_global_device_ids=true, to_apply=%region_6.0 | all-reduce | flops 1 | bytes 8 | tf_op jit(solution)/shard_map/psum | solution.py:53
  226.0 22.7 %psum.39 = f32[]{:T(128)} all-reduce(f32[]{:T(128)} %psum.38), channel_id=1, replica_groups=mesh['layer_0'=4,'layer_1'=2,'feat_0'=2,'feat_1'=8,'feat_2'=2] {'feat_2'}, use_global_device_ids=true, to_apply=%region_7.0 | all-reduce | flops 1 | bytes 8 | tf_op jit(solution)/shard_map/psum | solution.py:53
  249.4 20.9 %all-gather.2.cloned.1.call-done = bf16[512,2,2048]{2,0,1:T(8,128)(2,1)} async-done(((bf16[16,2,2048]{2,0,1:T(8,128)(2,1)}), bf16[512,2,2048]{2,0,1:T(8,128)(2,1)}) %all-gather.2.cloned.1.call-update) | async-done | bytes 4194320 | tf_op jit(solution)/shard_map/all_gather | solution.py:84
  270.3 3.7 %fusion.3 = f32[512,512]{1,0:T(8,128)S(1)} fusion(bf16[1,2,512,2048]{3,2,1,0:T(8,128)(2,1)} %param.10, bf16[512,2,2048]{2,0,1:T(8,128)(2,1)} %all-gather.2.cloned.1.call-done), kind=kOutput, calls=%fused_computation.11 | convolution fusion | flops 1073741824 | bytes 5242880 | tf_op jit(solution)/shard_map/td,fd->tf/dot_general | solution.py:94
  273.9 0.0 copy-done.1
  273.9 1.1 copy-done.3
  275.0 0.2 copy-done.8
  275.2 1.9 convert_reduce_fusion.1
  277.1 4.2 %fusion = bf16[1,2048,512]{1,2,0:T(8,128)(2,1)} fusion(bf16[512,512]{1,0:T(8,128)(2,1)S(1)} %get-tuple-element.20, bf16[512,2048]{1,0:T(8,128)(2,1)} %bitcast.1), kind=kOutput, calls=%fused_computation.6 | convolution fusion | flops 1074790400 | bytes 4718592 | tf_op jit(solution)/shard_map/td,tf->df/dot_general | solution.py:99
  281.3 3.9 %copy.14 = bf16[1,2048,512]{2,1,0:T(8,128)(2,1)} copy(bf16[1,2048,512]{1,2,0:T(8,128)(2,1)} %fusion) | data formatting | bytes 4194304
  285.2 3.0 %fusion.1 = bf16[1,512,2048]{2,1,0:T(8,128)(2,1)S(1)} fusion(bf16[512,512]{1,0:T(8,128)(2,1)S(1)} %get-tuple-element.17, bf16[512,2,2048]{2,0,1:T(8,128)(2,1)} %all-gather.2.cloned.1.call-done), kind=kOutput, calls=%fused_computation.7 | convolution fusion | flops 1074790400 | bytes 4718592 | tf_op jit(solution)/shard_map/tf,td->fd/dot_general | solution.py:90
  288.2 0.0 copy-done.4
  288.2 1.3 fusion.2
  289.5 2.4 maximum_bitcast_fusion
  291.9 1.0 convert_reduce_fusion
  (6 shorter events, 0.0 us)
Async XLA Ops:
  7.2 63.1 %copy-start = (bf16[1,2048,512]{2,1,0:T(8,128)(2,1)S(1)}, bf16[1,2048,512]{2,1,0:T(8,128)(2,1)}, u32[]{:S(2)}) copy-start(bf16[1,2048,512]{2,1,0:T(8,128)(2,1)} %param.8) | copy-start | bytes 6291460
  9.7 60.5 %all-to-all-start = ((bf16[32,16,2048]{2,1,0:T(8,128)(2,1)}), bf16[32,16,2048]{2,1,0:T(8,128)(2,1)}, u32[]{:S(2)}, u32[]{:S(2)}) async-start(bf16[32,16,2048]{2,1,0:T(8,128)(2,1)} %broadcast_in_dim.20), calls=%async_computation | async-start | bytes 4194304 | tf_op jit(solution)/shard_map/all_to_all | solution.py:15
  20.9 49.3 %copy-start.7 = (f32[1,512]{1,0:T(1,128)S(1)}, f32[1,512]{1,0:T(1,128)}, u32[]{:S(2)}) copy-start(f32[1,512]{1,0:T(1,128)} %param.9) | copy-start | bytes 6148
  20.9 81.0 %reduce-scatter.3.cloned.1.call-start = ((), (), s32[]{:S(2)}) async-start(), calls=%async_computation.3 | async-start | bytes 12582912 | tf_op jit(solution)/shard_map/reduce_scatter | solution.py:42
  70.2 4.0 %copy-start.2 = (bf16[1,2,512,2048]{2,3,1,0:T(8,128)(2,1)S(1)}, bf16[1,2,512,2048]{2,3,1,0:T(8,128)(2,1)}, u32[]{:S(2)}) copy-start(bf16[1,2,512,2048]{2,3,1,0:T(8,128)(2,1)} %copy.12) | copy-start | bytes 12582916
  80.4 95.6 %reduce-scatter.5.cloned.1.call-start = ((), (), s32[]{:S(2)}) async-start(), calls=%async_computation.4 | async-start | bytes 4456448 | tf_op jit(solution)/shard_map/reduce_scatter | solution.py:43
  102.0 82.6 %copy-start.5 = (bf16[1,16,2048]{2,1,0:T(8,128)(2,1)S(1)}, bf16[1,16,2048]{2,1,0:T(8,128)(2,1)}, u32[]{:S(2)}) copy-start(bf16[1,16,2048]{2,1,0:T(8,128)(2,1)} %param.7) | copy-start | bytes 196612
  102.0 82.6 %copy-start.6 = (f32[1,2048]{1,0:T(1,128)S(1)}, f32[1,2048]{1,0:T(1,128)}, u32[]{:S(2)}) copy-start(f32[1,2048]{1,0:T(1,128)} %param.11) | copy-start | bytes 24580
  102.0 168.2 %all-gather.2.cloned.1.call-start = ((), (), s32[]{:S(2)}) async-start(), calls=%async_computation.5 | async-start | bytes 4325376 | tf_op jit(solution)/shard_map/all_gather | solution.py:84
  176.9 7.7 %collective-permute-start = (f32[16,2048]{1,0:T(8,128)S(1)}, f32[16,2048]{1,0:T(8,128)S(1)}, u32[]{:S(2)}, u32[]{:S(2)}) collective-permute-start(f32[16,2048]{1,0:T(8,128)S(1)} %slice.25), channel_id=1, source_target_pairs={{0,32},{32,64},{64,96},{96,128},{128,160},{160,192},{192,224},{1,3... | collective-permute-start | bytes 393224 | tf_op jit(solution)/shard_map/ppermute | solution.py:49
  186.2 7.4 %collective-permute-start.1 = (bf16[16,2048]{1,0:T(8,128)(2,1)S(1)}, bf16[16,2048]{1,0:T(8,128)(2,1)S(1)}, u32[]{:S(2)}, u32[]{:S(2)}) collective-permute-start(bf16[16,2048]{1,0:T(8,128)(2,1)S(1)} %get-tuple-element.16), channel_id=1, source_target_pairs={{32,0},{64,32},{96,64},{128,96},{160,128},{192,160},{224,192},{33,... | collective-permute-start | bytes 196616 | tf_op jit(solution)/shard_map/ppermute | solution.py:49
  270.3 3.7 %copy-start.1 = (bf16[1,2,512,2048]{3,2,1,0:T(8,128)(2,1)S(1)}, bf16[1,2,512,2048]{3,2,1,0:T(8,128)(2,1)}, u32[]{:S(2)}) copy-start(bf16[1,2,512,2048]{3,2,1,0:T(8,128)(2,1)} %param.10) | copy-start | bytes 12582916
  270.3 4.7 %copy-start.3 = (bf16[512,2,2048]{2,0,1:T(8,128)(2,1)S(1)}, bf16[512,2,2048]{2,0,1:T(8,128)(2,1)}, u32[]{:S(2)}) copy-start(bf16[512,2,2048]{2,0,1:T(8,128)(2,1)} %all-gather.2.cloned.1.call-done) | copy-start | bytes 12582916
  270.3 4.9 %copy-start.8 = (f32[512,512]{1,0:T(8,128)S(1)}, f32[512,512]{1,0:T(8,128)}, u32[]{:S(2)}) copy-start(f32[512,512]{1,0:T(8,128)} %get-tuple-element.18) | copy-start | bytes 3145732
  285.2 3.0 %copy-start.4 = (bf16[512,2,2048]{2,0,1:T(8,128)(2,1)S(1)}, bf16[512,2,2048]{2,0,1:T(8,128)(2,1)}, u32[]{:S(2)}) copy-start(bf16[512,2,2048]{2,0,1:T(8,128)(2,1)} %all-gather.2.cloned.1.call-done) | copy-start | bytes 12582916
Sparse Core Ops, SparseCore 0:
  80.5 21.3 reduce-scatter.2
  104.5 71.4 reduce-scatter.4
  194.4 75.8 all-gather.1
where the time goes:
time: 301 us
  waiting for transfers between devices  169 us (56%)
  blocking collectives  54.5 us (18%)
  matrix products  20.4 us (7%)
  local copies, waits for them, and re-layouts  18.7 us (6%)
  starting transfers between devices  17 us (6%)
  between operations  15.6 us (5%)
  other arithmetic  5.57 us (2%)
    reduce_scatter x1, waiting for transfers between devices, scatter_pairs(): return lax.psum_scatter(tiles, chips, scatter_dimension=0, tiled=True)[0]  74 us
    psum x5, blocking collectives, one_axis_at_a_time(): return functools.reduce(lax.psum, axes, value)  54.5 us
    all_to_all x1, waiting for transfers between devices, copy_for_each(): lax.all_to_all(jnp.broadcast_to(value[None], (size, *value.shape)), axis,...  43 us
    reduce_scatter x1, waiting for transfers between devices, scatter_pairs(): tiles = lax.psum_scatter(tiles, core, scatter_dimension=0, tiled=True)  21.5 us
    all_gather x1, waiting for transfers between devices, shards(): gathered = lax.all_gather(stacked, FEAT, axis=0, tiled=True)  20.9 us
    unnamed x20, local copies, waits for them, and re-layouts  11.4 us
    all_to_all x1, starting transfers between devices, copy_for_each(): lax.all_to_all(jnp.broadcast_to(value[None], (size, *value.shape)), axis,...  11.2 us
    ppermute x2, waiting for transfers between devices, passed_along(): return lax.ppermute(block, axis, route)  9.36 us
  transfers between devices with their start and end apart: 6, of which 6 were waited for; matrix products, arithmetic and copies ran while one was open for 2% of the time, Pallas kernels for 0%

commit v1 on v0

--- a/solution.py
+++ b/solution.py
@@ -81,7 +81,9 @@
     offset = 1
     pieces.append(passed_along(grad, LAYER, -offset))
     stacked = jnp.stack(pieces, axis=1)
-    gathered = lax.all_gather(stacked, FEAT, axis=0, tiled=True)
+    gathered = jnp.concatenate(
+        lax.all_to_all(jnp.stack([stacked] * lax.axis_size(FEAT)), FEAT, 0, 0), axis=0
+    )
     fulls = [gathered[:, offset] for offset in range(reach)]
     dec_parts = []
     back = jnp.zeros(pre.shape, jnp.float32)

time: 301 us -> 355 us (1.18)
  blocking collectives: 54.5 us -> 108 us
  waiting for transfers between devices: 169 us -> 148 us
  starting transfers between devices: 17 us -> 32.8 us
  local copies, waits for them, and re-layouts: 18.7 us -> 22.6 us
    psum x5, blocking collectives: 54.5 us -> 108 us  [one_axis_at_a_time(): return functools.reduce(lax.psum, axes, value)]
    all_gather x1 -> x0, waiting for transfers between devices: 20.9 us -> none  [shards(): gathered = lax.all_gather(stacked, FEAT, axis=0, tiled=True)]
    all_to_all x0 -> x1, starting transfers between devices: none -> 16.4 us  [shards(): lax.all_to_all(jnp.stack([stacked] * lax.axis_size(FEAT)), FEAT, 0, 0)]
    unnamed x20 -> x16, local copies, waits for them, and re-layouts: 11.4 us -> 10.2 us
  transfers between devices with their start and end apart: 6 -> 6, of which waited for: 6 -> 5; matrix products, arithmetic and copies ran while one was open for 2% -> 2% of each run, Pallas kernels for 0% -> 0%
where the time goes in v1:
time: 355 us; the launch traced here: 354 us
  waiting for transfers between devices  148 us (42%)
  blocking collectives  108 us (30%)
  starting transfers between devices  32.8 us (9%)
  local copies, waits for them, and re-layouts  22.6 us (6%)
  matrix products  19 us (5%)
  between operations  15.9 us (4%)
  other arithmetic  7.16 us (2%)
    psum x5, blocking collectives, one_axis_at_a_time(): return functools.reduce(lax.psum, axes, value)  108 us
    reduce_scatter x1, waiting for transfers between devices, scatter_pairs(): return lax.psum_scatter(tiles, chips, scatter_dimension=0, tiled=True)[0]  74.1 us
    all_to_all x1, waiting for transfers between devices, copy_for_each(): lax.all_to_all(jnp.broadcast_to(value[None], (size, *value.shape)), axis,...  43 us
    reduce_scatter x1, waiting for transfers between devices, scatter_pairs(): tiles = lax.psum_scatter(tiles, core, scatter_dimension=0, tiled=True)  21.5 us
    all_to_all x1, starting transfers between devices, shards(): lax.all_to_all(jnp.stack([stacked] * lax.axis_size(FEAT)), FEAT, 0, 0)  16.4 us
    all_to_all x1, starting transfers between devices, copy_for_each(): lax.all_to_all(jnp.broadcast_to(value[None], (size, *value.shape)), axis,...  11.2 us
    unnamed x16, local copies, waits for them, and re-layouts  10.2 us
    ppermute x2, waiting for transfers between devices, passed_along(): return lax.ppermute(block, axis, route)  9.36 us
  transfers between devices with their start and end apart: 6, of which 5 were waited for; matrix products, arithmetic and copies ran while one was open for 2% of the time, Pallas kernels for 0%

profile of v1, /device:TPU:1, one launch (start us, length us, event | category | flops | bytes accessed | tf_op | source)
XLA Modules:
  0.0 353.5 jit_solution(1202267567992447423)
XLA Ops:
  7.2 0.0 copy-start
  7.2 2.6 broadcast_in_dim.20
  9.7 11.2 %all-to-all-start = ((bf16[32,16,2048]{2,1,0:T(8,128)(2,1)}), bf16[32,16,2048]{2,1,0:T(8,128)(2,1)}, u32[]{:S(2)}, u32[]{:S(2)}) async-start(bf16[32,16,2048]{2,1,0:T(8,128)(2,1)} %broadcast_in_dim.20), calls=%async_computation | async-start | bytes 4194304 | tf_op jit(solution)/shard_map/all_to_all | solution.py:15
  20.9 0.0 copy-start.5
  20.9 0.0 reduce-scatter.3.cloned.1.call-start
  21.0 6.2 %copy.16 = bf16[1,2,512,2048]{2,3,1,0:T(8,128)(2,1)} copy(bf16[1,2,512,2048]{3,2,1,0:T(8,128)(2,1)} %param.10) | data formatting | bytes 8388608 | tf_op args[4]
  27.2 43.0 %all-to-all-done = bf16[32,16,2048]{2,1,0:T(8,128)(2,1)} async-done(((bf16[32,16,2048]{2,1,0:T(8,128)(2,1)}), bf16[32,16,2048]{2,1,0:T(8,128)(2,1)}, u32[]{:S(2)}, u32[]{:S(2)}) %all-to-all-start) | async-done | bytes 2097184 | tf_op jit(solution)/shard_map/all_to_all | solution.py:15
  70.2 0.0 copy-done
  70.2 0.0 copy-done.5
  70.2 0.0 copy-start.2
  70.2 4.0 %multiply_convert_fusion = (bf16[512,512]{1,0:T(8,128)(2,1)S(1)}, f32[512,512]{1,0:T(8,128)}) fusion(f32[512]{0:T(512)S(1)} %bitcast.103, bf16[512,2048]{1,0:T(8,128)(2,1)} %bitcast.1, bf16[1,2048,512]{2,1,0:T(8,128)(2,1)S(1)} %copy-done), kind=kOutput, calls=%fused_computation.26 | convolution fusion | flops 1074790400 | bytes 5769216 | tf_op jit(solution)/shard_map/dot_general | solution.py:61
  74.2 0.0 copy-done.2
  74.2 2.4 convolution_bitcast_fusion
  76.6 3.8 %copy.17 = f32[2,16,16,4096]{3,2,1,0:T(8,128)} copy(f32[2,16,16,4096]{3,2,0,1:T(8,128)S(1)} %convolution_bitcast_fusion) | data formatting | bytes 16777216 | tf_op jit(solution)/shard_map/transpose | solution.py:41
  80.4 0.0 reduce-scatter.3.cloned.1.call-update
  80.4 0.0 reduce-scatter.5.cloned.1.call-start
  80.5 21.5 %reduce-scatter.3.cloned.1.call-done = f32[16,16,4096]{2,1,0:T(8,128)} async-done(((f32[32,16,4096]{2,1,0:T(8,128)}), f32[16,16,4096]{2,1,0:T(8,128)}) %reduce-scatter.3.cloned.1.call-update) | async-done | bytes 4194320 | tf_op jit(solution)/shard_map/reduce_scatter | solution.py:42
  102.0 0.0 copy-start.3
  102.0 0.0 reduce-scatter.5.cloned.1.call-update
  102.0 74.1 %reduce-scatter.5.cloned.1.call-done = f32[1,16,4096]{2,1,0:T(8,128)} async-done(((f32[16,16,4096]{2,1,0:T(8,128)}), f32[1,16,4096]{2,1,0:T(8,128)}) %reduce-scatter.5.cloned.1.call-update) | async-done | bytes 262160 | tf_op jit(solution)/shard_map/reduce_scatter | solution.py:43
  176.1 0.9 slice.25
  177.0 3.9 %collective-permute-start = (f32[16,2048]{1,0:T(8,128)S(1)}, f32[16,2048]{1,0:T(8,128)S(1)}, u32[]{:S(2)}, u32[]{:S(2)}) collective-permute-start(f32[16,2048]{1,0:T(8,128)S(1)} %slice.25), channel_id=1, source_target_pairs={{0,32},{32,64},{64,96},{96,128},{128,160},{160,192},{192,224},{1,3... | collective-permute-start | bytes 393224 | tf_op jit(solution)/shard_map/ppermute | solution.py:49
  180.9 3.3 collective-permute-done
  184.2 0.0 copy-done.3
  184.2 0.0 copy-done.4
  184.2 1.6 multiply_reduce_fusion
  185.8 1.3 collective-permute-start.1
  187.1 6.1 %collective-permute-done.1 = bf16[16,2048]{1,0:T(8,128)(2,1)S(1)} collective-permute-done((bf16[16,2048]{1,0:T(8,128)(2,1)S(1)}, bf16[16,2048]{1,0:T(8,128)(2,1)S(1)}, u32[]{:S(2)}, u32[]{:S(2)}) %collective-permute-start.1) | collective-permute-done | bytes 65568 | tf_op jit(solution)/shard_map/ppermute | solution.py:49
  193.1 2.5 stack.17
  195.7 16.4 %all-to-all-start.1 = ((bf16[32,16,2,2048]{3,1,2,0:T(8,128)(2,1)}), bf16[32,16,2,2048]{3,1,2,0:T(8,128)(2,1)}, u32[]{:S(2)}, u32[]{:S(2)}) async-start(bf16[32,16,2,2048]{3,1,2,0:T(8,128)(2,1)} %stack.17), calls=%async_computation.3 | async-start | bytes 8388608 | tf_op jit(solution)/shard_map/all_to_all | solution.py:85
  212.0 11.1 %psum.35 = f32[]{:T(128)} all-reduce(f32[]{:T(128)} %get-tuple-element.20), channel_id=1, replica_groups=mesh['layer_0'=4,'layer_1'=2,'feat_0'=2,'feat_1'=8,'feat_2'=2] {'layer_0'}, use_global_device_ids=true, to_apply=%region_3.0 | all-reduce | flops 1 | bytes 8 | tf_op jit(solution)/shard_map/psum | solution.py:53
  223.1 6.3 %psum.36 = f32[]{:T(128)} all-reduce(f32[]{:T(128)} %psum.35), channel_id=1, replica_groups=mesh['layer_0'=4,'layer_1'=2,'feat_0'=2,'feat_1'=8,'feat_2'=2] {'layer_1'}, use_global_device_ids=true, to_apply=%region_4.0 | all-reduce | flops 1 | bytes 8 | tf_op jit(solution)/shard_map/psum | solution.py:53
  229.4 5.2 %psum.37 = f32[]{:T(128)} all-reduce(f32[]{:T(128)} %psum.36), channel_id=1, replica_groups=mesh['layer_0'=4,'layer_1'=2,'feat_0'=2,'feat_1'=8,'feat_2'=2] {'feat_0'}, use_global_device_ids=true, to_apply=%region_5.0 | all-reduce | flops 1 | bytes 8 | tf_op jit(solution)/shard_map/psum | solution.py:53
  234.6 78.7 %psum.38 = f32[]{:T(128)} all-reduce(f32[]{:T(128)} %psum.37), channel_id=1, replica_groups=mesh['layer_0'=4,'layer_1'=2,'feat_0'=2,'feat_1'=8,'feat_2'=2] {'feat_1'}, use_global_device_ids=true, to_apply=%region_6.0 | all-reduce | flops 1 | bytes 8 | tf_op jit(solution)/shard_map/psum | solution.py:53
  313.3 6.8 %psum.39 = f32[]{:T(128)} all-reduce(f32[]{:T(128)} %psum.38), channel_id=1, replica_groups=mesh['layer_0'=4,'layer_1'=2,'feat_0'=2,'feat_1'=8,'feat_2'=2] {'feat_2'}, use_global_device_ids=true, to_apply=%region_7.0 | all-reduce | flops 1 | bytes 8 | tf_op jit(solution)/shard_map/psum | solution.py:53
  320.7 0.0 all-to-all-done.1
  320.7 0.0 copy-start.1
  320.8 2.7 copy.18
  323.4 1.0 convert_reduce_fusion
  324.4 0.0 copy-done.1
  324.4 1.3 fusion.3
  325.7 2.6 fusion.1
  328.3 2.6 fusion.2
  330.9 0.0 copy-done.6
  330.9 1.9 convert_reduce_fusion.1
  332.8 4.2 %fusion = bf16[1,2048,512]{1,2,0:T(8,128)(2,1)} fusion(bf16[512,512]{1,0:T(8,128)(2,1)S(1)} %get-tuple-element.25, bf16[512,2048]{1,0:T(8,128)(2,1)} %bitcast.1), kind=kOutput, calls=%fused_computation.6 | convolution fusion | flops 1074790400 | bytes 4718592 | tf_op jit(solution)/shard_map/td,tf->df/dot_general | solution.py:101
  337.0 3.9 %copy.19 = bf16[1,2048,512]{2,1,0:T(8,128)(2,1)} copy(bf16[1,2048,512]{1,2,0:T(8,128)(2,1)} %fusion) | data formatting | bytes 4194304
  340.9 4.6 %maximum_bitcast_fusion = bf16[1,2,512,2048]{3,2,1,0:T(8,128)(2,1)} fusion(bf16[1,512,2048]{2,1,0:T(8,128)(2,1)} %fusion.2, bf16[1,512,2048]{2,1,0:T(8,128)(2,1)} %fusion.1), kind=kLoop, calls=%fused_computation.1 | loop fusion | flops 2097152 | bytes 8388608 | tf_op jit(solution)/shard_map/broadcast_in_dim | solution.py:106
  (3 shorter events, 0.0 us)
Async XLA Ops:
  7.2 63.1 %copy-start = (bf16[1,2048,512]{2,1,0:T(8,128)(2,1)S(1)}, bf16[1,2048,512]{2,1,0:T(8,128)(2,1)}, u32[]{:S(2)}) copy-start(bf16[1,2048,512]{2,1,0:T(8,128)(2,1)} %param.8) | copy-start | bytes 6291460
  9.7 60.5 %all-to-all-start = ((bf16[32,16,2048]{2,1,0:T(8,128)(2,1)}), bf16[32,16,2048]{2,1,0:T(8,128)(2,1)}, u32[]{:S(2)}, u32[]{:S(2)}) async-start(bf16[32,16,2048]{2,1,0:T(8,128)(2,1)} %broadcast_in_dim.20), calls=%async_computation | async-start | bytes 4194304 | tf_op jit(solution)/shard_map/all_to_all | solution.py:15
  20.9 49.3 %copy-start.5 = (f32[1,512]{1,0:T(1,128)S(1)}, f32[1,512]{1,0:T(1,128)}, u32[]{:S(2)}) copy-start(f32[1,512]{1,0:T(1,128)} %param.9) | copy-start | bytes 6148
  20.9 81.0 %reduce-scatter.3.cloned.1.call-start = ((), (), s32[]{:S(2)}) async-start(), calls=%async_computation.4 | async-start | bytes 12582912 | tf_op jit(solution)/shard_map/reduce_scatter | solution.py:42
  70.2 4.0 %copy-start.2 = (bf16[1,2,512,2048]{2,3,1,0:T(8,128)(2,1)S(1)}, bf16[1,2,512,2048]{2,3,1,0:T(8,128)(2,1)}, u32[]{:S(2)}) copy-start(bf16[1,2,512,2048]{2,3,1,0:T(8,128)(2,1)} %copy.16) | copy-start | bytes 12582916
  80.4 95.7 %reduce-scatter.5.cloned.1.call-start = ((), (), s32[]{:S(2)}) async-start(), calls=%async_computation.5 | async-start | bytes 4456448 | tf_op jit(solution)/shard_map/reduce_scatter | solution.py:43
  102.0 82.2 %copy-start.3 = (bf16[1,16,2048]{2,1,0:T(8,128)(2,1)S(1)}, bf16[1,16,2048]{2,1,0:T(8,128)(2,1)}, u32[]{:S(2)}) copy-start(bf16[1,16,2048]{2,1,0:T(8,128)(2,1)} %param.7) | copy-start | bytes 196612
  102.0 82.2 %copy-start.4 = (f32[1,2048]{1,0:T(1,128)S(1)}, f32[1,2048]{1,0:T(1,128)}, u32[]{:S(2)}) copy-start(f32[1,2048]{1,0:T(1,128)} %param.11) | copy-start | bytes 24580
  177.0 7.2 %collective-permute-start = (f32[16,2048]{1,0:T(8,128)S(1)}, f32[16,2048]{1,0:T(8,128)S(1)}, u32[]{:S(2)}, u32[]{:S(2)}) collective-permute-start(f32[16,2048]{1,0:T(8,128)S(1)} %slice.25), channel_id=1, source_target_pairs={{0,32},{32,64},{64,96},{96,128},{128,160},{160,192},{192,224},{1,3... | collective-permute-start | bytes 393224 | tf_op jit(solution)/shard_map/ppermute | solution.py:49
  185.8 7.4 %collective-permute-start.1 = (bf16[16,2048]{1,0:T(8,128)(2,1)S(1)}, bf16[16,2048]{1,0:T(8,128)(2,1)S(1)}, u32[]{:S(2)}, u32[]{:S(2)}) collective-permute-start(bf16[16,2048]{1,0:T(8,128)(2,1)S(1)} %get-tuple-element.21), channel_id=1, source_target_pairs={{32,0},{64,32},{96,64},{128,96},{160,128},{192,160},{224,192},{33,... | collective-permute-start | bytes 196616 | tf_op jit(solution)/shard_map/ppermute | solution.py:49
  195.7 125.1 %all-to-all-start.1 = ((bf16[32,16,2,2048]{3,1,2,0:T(8,128)(2,1)}), bf16[32,16,2,2048]{3,1,2,0:T(8,128)(2,1)}, u32[]{:S(2)}, u32[]{:S(2)}) async-start(bf16[32,16,2,2048]{3,1,2,0:T(8,128)(2,1)} %stack.17), calls=%async_computation.3 | async-start | bytes 8388608 | tf_op jit(solution)/shard_map/all_to_all | solution.py:85
  320.7 3.6 %copy-start.1 = (bf16[1,2,512,2048]{3,2,1,0:T(8,128)(2,1)S(1)}, bf16[1,2,512,2048]{3,2,1,0:T(8,128)(2,1)}, u32[]{:S(2)}) copy-start(bf16[1,2,512,2048]{3,2,1,0:T(8,128)(2,1)} %param.10) | copy-start | bytes 12582916
  328.3 2.6 copy-start.6
Sparse Core Ops, SparseCore 0:
  80.5 21.3 reduce-scatter.2
  104.5 71.4 reduce-scatter.4
